TPU v7x, 32 devices: a whole 2x2x4 slice. The times are simulated.
32 devices in a mesh: tm: 4 (over z), space: 8 (over y, x, core).
Axes of the slice: x: 2, y: 2, z: 4, core: 2. Of those that a mesh axis runs over, the one named last changes fastest.
Arguments:
- labels: int32 [32, 64, 256], P('space'), may hold values from 0 to 3
- conductivity: float32 [4], replicated, may hold values from 0.02 to 1
- coil_pattern: float32 [3, 32, 64, 256], P(None, 'space'), may hold values from -18 to 18
- currents: float32 [4, 2, 3], P('tm'), may hold values from -4 to 4
- initial_state: float32 [32, 64, 256], P('space'), may hold values from -6 to 6
Outputs:
- slice_starts: float32 [4, 32, 64, 256], P('tm', 'space')
- fine_ends: float32 [4, 32, 64, 256], P('tm', 'space')
All inputs are finite; a program needn't handle non-finite values.
Results may differ from a plain program's by a relative error of at most 0.00021.
Values sent between devices are 32-bit elements; how exact they have to be, the bound alone decides.
A program may use at most 64 MiB of HBM per device.

v0:
```python
import jax
import jax.numpy as jnp
from jax import lax
from jax.sharding import PartitionSpec as P

REGIONS = 4
PHASES = 3
FINE_STEPS = 2
CG_FINE = 2
CG_COARSE = 4
PARA_ITERS = 2


def with_halo(x, sides, width):
    for axis, dim in sides:
        count, length = (lax.axis_size(axis), x.shape[dim])
        up = [(i, (i + 1) % count) for i in range(count - 1)]
        down = [(j, i) for i, j in up]
        last = lax.slice_in_dim(x, length - width, length, axis=dim)
        initial = lax.slice_in_dim(x, 0, width, axis=dim)
        before = lax.ppermute(last, axis, up)
        after = lax.ppermute(initial, axis, down)
        x = jnp.concatenate([before, x, after], axis=dim)
    return x


def from_behind(value, axis, steps):
    count = lax.axis_size(axis)
    pairs = [(source, (source + steps) % count) for source in range(count)]
    return lax.ppermute(value, axis, pairs)


def restrict(volume):
    first_dim, second_dim, third_dim = volume.shape
    blocks = volume.reshape(first_dim // 4, 4, second_dim // 4, 4, third_dim // 4, 4)
    return jnp.mean(blocks, axis=(1, 3, 5))


def prolong(coarse_field):
    first_dim, second_dim, third_dim = coarse_field.shape
    spread = jnp.broadcast_to(
        coarse_field[:, None, :, None, :, None], (first_dim, 4, second_dim, 4, third_dim, 4)
    )
    return spread.reshape(first_dim * 4, second_dim * 4, third_dim * 4)


def neighbours(padded):
    summed = padded[2:, 1:-1, 1:-1] + padded[:-2, 1:-1, 1:-1]
    summed = summed + padded[1:-1, 2:, 1:-1] + padded[1:-1, :-2, 1:-1]
    return summed + padded[1:-1, 1:-1, 2:] + padded[1:-1, 1:-1, :-2]


def fine_operator(volume, weight):
    padded = with_halo(volume, (("space", 0),), 1)
    padded = jnp.pad(padded, ((0, 0), (1, 1), (1, 1)))
    beside = neighbours(padded)
    return weight * volume + (6.0 * volume - beside)


def coarse_operator(volume, weight):
    beside = neighbours(jnp.pad(volume, 1))
    return weight * volume + 0.0625 * (6.0 * volume - beside)


def conjugate(operator, right_side, guess, count):
    solution = guess
    residual = right_side - operator(solution)
    direction = residual
    res_norm = jnp.sum(residual * residual)
    for sweep_step in range(count):
        applied = operator(direction)
        step_len = res_norm / jnp.sum(direction * applied)
        solution = solution + step_len * direction
        residual = residual - step_len * applied
        if sweep_step + 1 < count:
            new_norm = jnp.sum(residual * residual)
            direction = residual + new_norm / res_norm * direction
            res_norm = new_norm
    return solution


def paired_sums(residual, applied):
    return lax.psum((jnp.sum(residual * residual), jnp.sum(residual * applied)), "space")


def fine_solve(right_side, guess, weight):
    solution = guess
    residual = right_side - fine_operator(solution, weight)
    applied = fine_operator(residual, weight)
    res_norm, product = paired_sums(residual, applied)
    step_len = res_norm / product
    direction, applied_dir = (residual, applied)
    for sweep_step in range(CG_FINE):
        solution = solution + step_len * direction
        residual = residual - step_len * applied_dir
        if sweep_step + 1 < CG_FINE:
            applied = fine_operator(residual, weight)
            new_norm, product = paired_sums(residual, applied)
            ratio = new_norm / res_norm
            step_len = new_norm / (product - ratio * new_norm / step_len)
            direction = residual + ratio * direction
            applied_dir = applied + ratio * applied_dir
            res_norm = new_norm
    return solution


def coarse_sweep(coarse_begin, correction, weight_coarse, source_coarse):
    slice_index = lax.axis_index("tm")
    slices = lax.axis_size("tm")

    def advance(vector_in):
        right_side = weight_coarse * vector_in + source_coarse
        return conjugate(
            lambda inner_vec: coarse_operator(inner_vec, weight_coarse),
            right_side,
            vector_in,
            CG_COARSE,
        )

    def keep_same(vector_in):
        return vector_in

    def one_turn(turn_index, loop_state):
        current, used_start, advanced = loop_state
        active = slice_index == turn_index
        stepped = lax.cond(active, advance, keep_same, current)
        outgoing = stepped + correction
        arrived = from_behind(outgoing, "tm", 1)
        receiver = slice_index == (turn_index + 1) % slices
        used_start = jnp.where(active, current, used_start)
        advanced = jnp.where(active, stepped, advanced)
        current = jnp.where(receiver, arrived, current)
        return (current, used_start, advanced)

    return lax.fori_loop(0, slices, one_turn, (coarse_begin, coarse_begin, coarse_begin))


def body(labels, conductivity, coil_pattern, currents, initial_state):
    sigma_cell = jnp.where(labels == 0, conductivity[0], 0.0)
    for region in range(1, REGIONS):
        sigma_cell = sigma_cell + jnp.where(labels == region, conductivity[region], 0.0)
    coarse_pattern = jnp.stack(
        [restrict(coil_pattern[phase_index]) for phase_index in range(PHASES)]
    )
    start_coarse, sigma_coarse, coils_coarse = (
        lax.all_gather(restrict(initial_state), "space", axis=0, tiled=True),
        lax.all_gather(restrict(sigma_cell), "space", axis=0, tiled=True),
        lax.all_gather(coarse_pattern, "space", axis=1, tiled=True),
    )
    slice_currents = currents[0]
    mean_current = jnp.mean(slice_currents, axis=0)
    source_coarse = mean_current[0] * coils_coarse[0]
    for phase_index in range(1, PHASES):
        source_coarse = source_coarse + mean_current[phase_index] * coils_coarse[phase_index]
    weight_coarse = sigma_coarse / float(FINE_STEPS)
    is_first = lax.axis_index("tm") == 0
    space_index = lax.axis_index("space")
    plane_count = initial_state.shape[0] // 4

    def own_share(whole_field):
        return lax.dynamic_slice_in_dim(whole_field, space_index * plane_count, plane_count, 0)

    earlier = initial_state - prolong(restrict(initial_state))
    latest = jnp.zeros_like(initial_state)
    correction = jnp.zeros_like(start_coarse)
    coarse_begin = start_coarse
    slice_state = initial_state
    fine_state = initial_state
    for para_index in range(PARA_ITERS + 1):
        landed, used_start, advanced = coarse_sweep(
            coarse_begin, correction, weight_coarse, source_coarse
        )
        slice_state = prolong(own_share(used_start)) + jnp.where(is_first, earlier, latest)
        if para_index < PARA_ITERS:
            volume = slice_state
            for step_index in range(FINE_STEPS):
                source = slice_currents[step_index, 0] * coil_pattern[0]
                for phase_index in range(1, PHASES):
                    source = (
                        source + slice_currents[step_index, phase_index] * coil_pattern[phase_index]
                    )
                volume = fine_solve(sigma_cell * volume + source, volume, sigma_cell)
            fine_state = volume
            fine_coarse = restrict(fine_state)
            correction = lax.all_gather(
                fine_coarse - own_share(advanced), "space", axis=0, tiled=True
            )
            arrived_rest = from_behind(fine_state - prolong(fine_coarse), "tm", 1)
            earlier, latest = (latest, arrived_rest)
            coarse_begin = landed
    return (slice_state[None], fine_state[None])


def solution(mesh):
    in_specs = (
        P("space", None, None),
        P(),
        P(None, "space", None, None),
        P("tm", None, None),
        P("space", None, None),
    )
    out_specs = (P("tm", "space", None, None), P("tm", "space", None, None))
    return jax.shard_map(body, mesh=mesh, in_specs=in_specs, out_specs=out_specs, check_vma=False)
```

profile of v0, /device:TPU:0, one launch (start us, length us, event | category | flops | bytes accessed | tf_op | source)
XLA Modules:
  0.0 569.8 jit_solution(4167194194046604532)
XLA Ops:
  4.0 10.7 %all-gather = f32[128,64]{1,0:T(8,128)S(1)} all-gather(f32[16,64]{1,0:T(8,128)S(1)} %broadcast_multiply_fusion.4), channel_id=2, replica_groups=mesh['tm'=4,'space'=8] {'space'}, dimensions={0}, use_global_device_ids=true | all-gather | bytes 36864 | tf_op jit(solution)/shard_map/all_gather | solution.py:146
  22.5 9.2 %all-gather.1 = f32[128,64]{1,0:T(8,128)S(1)} all-gather(f32[16,64]{1,0:T(8,128)S(1)} %broadcast_multiply_fusion.3), channel_id=3, replica_groups=mesh['tm'=4,'space'=8] {'space'}, dimensions={0}, use_global_device_ids=true | all-gather | bytes 36864 | tf_op jit(solution)/shard_map/all_gather | solution.py:147
  40.6 8.5 %all_gather.17 = f32[3,8,16,64]{3,2,1,0:T(8,128)S(1)} all-gather(f32[3,1,16,64]{3,2,1,0:T(8,128)S(1)} %pad_maximum_fusion.24), channel_id=1, replica_groups=mesh['tm'=4,'space'=8] {'space'}, dimensions={1}, use_global_device_ids=true | all-gather | bytes 110592 | tf_op jit(solution)/shard_map/all_gather | solution.py:148
  51.5 69.4 %while.64 = (s32[]{:T(128)}, f32[8,16,64]{2,1,0:T(8,128)S(1)}, f32[8,16,64]{2,1,0:T(8,128)S(1)}, f32[8,16,64]{2,1,0:T(8,128)S(1)}, s32[]{:T(128)}, /*index=5*/f3...) while((s32[]{:T(128)}, f32[8,16,64]{2,1,0:T(8,128)S(1)}, ...), condition=%wide.region_22.23_spmd, body=%wide.region_11.22_spmd.sunk | while | flops 827407 | bytes 1704424 | solution.py:135
  51.5 13.7 %conditional.6 = (f32[8,16,64]{2,1,0:T(8,128)S(1)}) conditional(s32[]{:T(128)} %convert_element_type.62, f32[8,16,64]{2,1,0:T(8,128)S(1)} %get-tuple-element.954, (f32[8,16,64]{2,1,0:T(8,128)S(1)}, f32[8,16,64]{2,1,0:T(8,128)S(1)}, f32[8,16,64]{2,1,0:T(8,128)S(1)}) %tuple.207), branch_computations={%region_12.12_spmd, %region_13.21_spmd} | conditional | flops 802815 | bytes 1310900 | solution.py:126
  65.3 6.1 %collective-permute-done = f32[8,16,64]{2,1,0:T(8,128)S(1)} collective-permute-done((f32[8,16,64]{2,1,0:T(8,128)S(1)}, f32[8,16,64]{2,1,0:T(8,128)S(1)}, u32[]{:S(2)}, u32[]{:S(2)}) %collective-permute-start) | collective-permute-done | bytes 32800 | tf_op jit(solution)/shard_map/while/body/eval_jaxpr/ppermute | solution.py:30
  71.5 12.2 %collective-permute-start = (f32[8,16,64]{2,1,0:T(8,128)S(1)}, f32[8,16,64]{2,1,0:T(8,128)S(1)}, u32[]{:S(2)}, u32[]{:S(2)}) collective-permute-start(f32[8,16,64]{2,1,0:T(8,128)S(1)} %get-tuple-element.1044), channel_id=1, source_target_pairs={{0,8},{8,16},{16,24},{24,0},{1,9},{9,17},{17,25},{25,1},{2,10},{10... | collective-permute-start | bytes 98312 | tf_op jit(solution)/shard_map/while/body/eval_jaxpr/ppermute | solution.py:30
  88.1 3.7 collective-permute-done
  91.9 11.9 %collective-permute-start = (f32[8,16,64]{2,1,0:T(8,128)S(1)}, f32[8,16,64]{2,1,0:T(8,128)S(1)}, u32[]{:S(2)}, u32[]{:S(2)}) collective-permute-start(f32[8,16,64]{2,1,0:T(8,128)S(1)} %get-tuple-element.1044), channel_id=1, source_target_pairs={{0,8},{8,16},{16,24},{24,0},{1,9},{9,17},{17,25},{25,1},{2,10},{10... | collective-permute-start | bytes 98312 | tf_op jit(solution)/shard_map/while/body/eval_jaxpr/ppermute | solution.py:30
  103.8 17.1 %collective-permute-done = f32[8,16,64]{2,1,0:T(8,128)S(1)} collective-permute-done((f32[8,16,64]{2,1,0:T(8,128)S(1)}, f32[8,16,64]{2,1,0:T(8,128)S(1)}, u32[]{:S(2)}, u32[]{:S(2)}) %collective-permute-start) | collective-permute-done | bytes 32800 | tf_op jit(solution)/shard_map/while/body/eval_jaxpr/ppermute | solution.py:30
  128.7 5.5 fusion.178
  135.5 4.1 collective-permute-start.6
  140.7 3.5 multiply_reduce_fusion.31
  144.2 15.3 %all-reduce.34 = (f32[]{:T(128)}, f32[]{:T(128)}) all-reduce(f32[]{:T(128)} %get-tuple-element.650, f32[]{:T(128)} %get-tuple-element.649), channel_id=1, replica_groups=mesh['tm'=4,'space'=8] {'space'}, use_global_device_ids=true, to_apply=%region_24.25 | all-reduce | flops 2 | bytes 16 | tf_op jit(solution)/shard_map/psum | solution.py:83
  166.3 3.6 fusion.171
  169.9 16.9 %all-reduce.33 = (f32[]{:T(128)}, f32[]{:T(128)}) all-reduce(f32[]{:T(128)} %get-tuple-element.648, f32[]{:T(128)} %get-tuple-element.647), channel_id=1, replica_groups=mesh['tm'=4,'space'=8] {'space'}, use_global_device_ids=true, to_apply=%region_28.29 | all-reduce | flops 2 | bytes 16 | tf_op jit(solution)/shard_map/psum | solution.py:83
  196.8 5.5 fusion.166
  203.6 4.4 collective-permute-start.12
  209.1 3.5 multiply_reduce_fusion.28
  212.6 17.1 %all-reduce.32 = (f32[]{:T(128)}, f32[]{:T(128)}) all-reduce(f32[]{:T(128)} %get-tuple-element.646, f32[]{:T(128)} %get-tuple-element.645), channel_id=1, replica_groups=mesh['tm'=4,'space'=8] {'space'}, use_global_device_ids=true, to_apply=%region_32.33 | all-reduce | flops 2 | bytes 16 | tf_op jit(solution)/shard_map/psum | solution.py:83
  236.6 3.5 fusion.159
  240.1 16.3 %all-reduce.31 = (f32[]{:T(128)}, f32[]{:T(128)}) all-reduce(f32[]{:T(128)} %get-tuple-element.644, f32[]{:T(128)} %get-tuple-element.643), channel_id=1, replica_groups=mesh['tm'=4,'space'=8] {'space'}, use_global_device_ids=true, to_apply=%region_36.37 | all-reduce | flops 2 | bytes 16 | tf_op jit(solution)/shard_map/psum | solution.py:83
  265.9 10.6 %all_gather.18 = f32[8,16,64]{2,1,0:T(8,128)S(1)} all-gather(f32[1,16,64]{2,1,0:T(8,128)S(1)} %bitcast_subtract_fusion.1), channel_id=1, replica_groups=mesh['tm'=4,'space'=8] {'space'}, dimensions={0}, use_global_device_ids=true | all-gather | bytes 36864 | tf_op jit(solution)/shard_map/all_gather | solution.py:185
  276.5 72.3 %while.65 = (s32[]{:T(128)}, f32[8,16,64]{2,1,0:T(8,128)S(1)}, f32[8,16,64]{2,1,0:T(8,128)S(1)}, f32[8,16,64]{2,1,0:T(8,128)S(1)}, s32[]{:T(128)}, /*index=5*/f3...) while((s32[]{:T(128)}, f32[8,16,64]{2,1,0:T(8,128)S(1)}, ...), condition=%wide.region_52.53_spmd, body=%wide.region_41.52_spmd.sunk | while | flops 835599 | bytes 1769968 | solution.py:135
  276.5 14.3 %conditional.7 = (f32[8,16,64]{2,1,0:T(8,128)S(1)}) conditional(s32[]{:T(128)} %convert_element_type.63, f32[8,16,64]{2,1,0:T(8,128)S(1)} %get-tuple-element.988, (f32[8,16,64]{2,1,0:T(8,128)S(1)}, f32[8,16,64]{2,1,0:T(8,128)S(1)}, f32[8,16,64]{2,1,0:T(8,128)S(1)}) %tuple.211), branch_computations={%region_42.42_spmd, %region_43.51_spmd} | conditional | flops 802815 | bytes 1310900 | solution.py:126
  290.9 6.1 %collective-permute-done.1 = f32[8,16,64]{2,1,0:T(8,128)S(1)} collective-permute-done((f32[8,16,64]{2,1,0:T(8,128)S(1)}, f32[8,16,64]{2,1,0:T(8,128)S(1)}, u32[]{:S(2)}, u32[]{:S(2)}) %collective-permute-start.1) | collective-permute-done | bytes 32800 | tf_op jit(solution)/shard_map/while/body/eval_jaxpr/ppermute | solution.py:30
  297.2 12.9 %collective-permute-start.1 = (f32[8,16,64]{2,1,0:T(8,128)S(1)}, f32[8,16,64]{2,1,0:T(8,128)S(1)}, u32[]{:S(2)}, u32[]{:S(2)}) collective-permute-start(f32[8,16,64]{2,1,0:T(8,128)S(1)} %get-tuple-element.929), channel_id=1, source_target_pairs={{0,8},{8,16},{16,24},{24,0},{1,9},{9,17},{17,25},{25,1},{2,10},{10... | collective-permute-start | bytes 98312 | tf_op jit(solution)/shard_map/while/body/eval_jaxpr/ppermute | solution.py:30
  314.5 3.7 collective-permute-done.1
  318.3 12.6 %collective-permute-start.1 = (f32[8,16,64]{2,1,0:T(8,128)S(1)}, f32[8,16,64]{2,1,0:T(8,128)S(1)}, u32[]{:S(2)}, u32[]{:S(2)}) collective-permute-start(f32[8,16,64]{2,1,0:T(8,128)S(1)} %get-tuple-element.929), channel_id=1, source_target_pairs={{0,8},{8,16},{16,24},{24,0},{1,9},{9,17},{17,25},{25,1},{2,10},{10... | collective-permute-start | bytes 98312 | tf_op jit(solution)/shard_map/while/body/eval_jaxpr/ppermute | solution.py:30
  330.9 17.8 %collective-permute-done.1 = f32[8,16,64]{2,1,0:T(8,128)S(1)} collective-permute-done((f32[8,16,64]{2,1,0:T(8,128)S(1)}, f32[8,16,64]{2,1,0:T(8,128)S(1)}, u32[]{:S(2)}, u32[]{:S(2)}) %collective-permute-start.1) | collective-permute-done | bytes 32800 | tf_op jit(solution)/shard_map/while/body/eval_jaxpr/ppermute | solution.py:30
  364.7 3.5 multiply_reduce_fusion.25
  368.2 16.2 %all-reduce.30 = (f32[]{:T(128)}, f32[]{:T(128)}) all-reduce(f32[]{:T(128)} %get-tuple-element.642, f32[]{:T(128)} %get-tuple-element.641), channel_id=1, replica_groups=mesh['tm'=4,'space'=8] {'space'}, use_global_device_ids=true, to_apply=%region_54.55 | all-reduce | flops 2 | bytes 16 | tf_op jit(solution)/shard_map/psum | solution.py:83
  391.3 3.6 fusion.147
  394.9 15.6 %all-reduce.29 = (f32[]{:T(128)}, f32[]{:T(128)}) all-reduce(f32[]{:T(128)} %get-tuple-element.640, f32[]{:T(128)} %get-tuple-element.639), channel_id=1, replica_groups=mesh['tm'=4,'space'=8] {'space'}, use_global_device_ids=true, to_apply=%region_58.59 | all-reduce | flops 2 | bytes 16 | tf_op jit(solution)/shard_map/psum | solution.py:83
  424.7 4.4 collective-permute-start.25
  430.2 3.5 multiply_reduce_fusion.22
  433.7 17.1 %all-reduce.28 = (f32[]{:T(128)}, f32[]{:T(128)}) all-reduce(f32[]{:T(128)} %get-tuple-element.638, f32[]{:T(128)} %get-tuple-element.637), channel_id=1, replica_groups=mesh['tm'=4,'space'=8] {'space'}, use_global_device_ids=true, to_apply=%region_62.63 | all-reduce | flops 2 | bytes 16 | tf_op jit(solution)/shard_map/psum | solution.py:83
  453.5 3.3 collective-permute-start.27
  457.6 3.5 fusion.135
  461.1 16.2 %all-reduce.27 = (f32[]{:T(128)}, f32[]{:T(128)}) all-reduce(f32[]{:T(128)} %get-tuple-element.636, f32[]{:T(128)} %get-tuple-element.635), channel_id=1, replica_groups=mesh['tm'=4,'space'=8] {'space'}, use_global_device_ids=true, to_apply=%region_66.67 | all-reduce | flops 2 | bytes 16 | tf_op jit(solution)/shard_map/psum | solution.py:83
  486.4 10.6 %all_gather.19 = f32[8,16,64]{2,1,0:T(8,128)S(1)} all-gather(f32[1,16,64]{2,1,0:T(8,128)S(1)} %bitcast_subtract_fusion), channel_id=1, replica_groups=mesh['tm'=4,'space'=8] {'space'}, dimensions={0}, use_global_device_ids=true | all-gather | bytes 36864 | tf_op jit(solution)/shard_map/all_gather | solution.py:185
  497.0 69.5 %while.66 = (s32[]{:T(128)}, f32[8,16,64]{2,1,0:T(8,128)S(1)}, f32[8,16,64]{2,1,0:T(8,128)S(1)}, s32[]{:T(128)}, f32[8,16,64]{2,1,0:T(8,128)S(1)}, /*index=5*/f3...) while((s32[]{:T(128)}, f32[8,16,64]{2,1,0:T(8,128)S(1)}, ...), condition=%wide.region_82.83_spmd, body=%wide.region_71.82_spmd.sunk | while | flops 827407 | bytes 1704423 | solution.py:135
  497.0 13.7 %conditional.8 = (f32[8,16,64]{2,1,0:T(8,128)S(1)}) conditional(s32[]{:T(128)} %convert_element_type.64, f32[8,16,64]{2,1,0:T(8,128)S(1)} %get-tuple-element.1023, (f32[8,16,64]{2,1,0:T(8,128)S(1)}, f32[8,16,64]{2,1,0:T(8,128)S(1)}, f32[8,16,64]{2,1,0:T(8,128)S(1)}) %tuple.214), branch_computations={%region_72.72_spmd, %region_73.81_spmd} | conditional | flops 802815 | bytes 1310900 | solution.py:126
  510.8 6.1 %collective-permute-done.2 = f32[8,16,64]{2,1,0:T(8,128)S(1)} collective-permute-done((f32[8,16,64]{2,1,0:T(8,128)S(1)}, f32[8,16,64]{2,1,0:T(8,128)S(1)}, u32[]{:S(2)}, u32[]{:S(2)}) %collective-permute-start.2) | collective-permute-done | bytes 32800 | tf_op jit(solution)/shard_map/while/body/eval_jaxpr/ppermute | solution.py:30
  517.0 12.2 %collective-permute-start.2 = (f32[8,16,64]{2,1,0:T(8,128)S(1)}, f32[8,16,64]{2,1,0:T(8,128)S(1)}, u32[]{:S(2)}, u32[]{:S(2)}) collective-permute-start(f32[8,16,64]{2,1,0:T(8,128)S(1)} %add.2463), channel_id=1, source_target_pairs={{0,8},{8,16},{16,24},{24,0},{1,9},{9,17},{17,25},{25,1},{2,10},{10... | collective-permute-start | bytes 98312 | tf_op jit(solution)/shard_map/while/body/eval_jaxpr/ppermute | solution.py:30
  533.7 3.7 collective-permute-done.2
  537.5 11.9 %collective-permute-start.2 = (f32[8,16,64]{2,1,0:T(8,128)S(1)}, f32[8,16,64]{2,1,0:T(8,128)S(1)}, u32[]{:S(2)}, u32[]{:S(2)}) collective-permute-start(f32[8,16,64]{2,1,0:T(8,128)S(1)} %add.2463), channel_id=1, source_target_pairs={{0,8},{8,16},{16,24},{24,0},{1,9},{9,17},{17,25},{25,1},{2,10},{10... | collective-permute-start | bytes 98312 | tf_op jit(solution)/shard_map/while/body/eval_jaxpr/ppermute | solution.py:30
  549.4 17.1 %collective-permute-done.2 = f32[8,16,64]{2,1,0:T(8,128)S(1)} collective-permute-done((f32[8,16,64]{2,1,0:T(8,128)S(1)}, f32[8,16,64]{2,1,0:T(8,128)S(1)}, u32[]{:S(2)}, u32[]{:S(2)}) %collective-permute-start.2) | collective-permute-done | bytes 32800 | tf_op jit(solution)/shard_map/while/body/eval_jaxpr/ppermute | solution.py:30
  (247 shorter events, 127.0 us)
Async XLA Ops:
  14.8 2.0 copy-start.9
  14.8 2.7 copy-start
  20.1 11.6 %copy-start.1 = (f32[3,4,64,256]{3,2,1,0:T(8,128)S(1)}, f32[3,4,64,256]{3,2,1,0:T(8,128)}, u32[]{:S(2)}) copy-start(f32[3,4,64,256]{3,2,1,0:T(8,128)} %param.19) | copy-start | bytes 2359300
  32.5 3.3 copy-start.7
  38.1 10.9 %copy-start.8 = (f32[1,2,3]{2,1,0:T(2,128)S(1)}, f32[1,2,3]{2,1,0:T(2,128)}, u32[]{:S(2)}) copy-start(f32[1,2,3]{2,1,0:T(2,128)} %param.20) | copy-start | bytes 76
  65.2 6.2 %collective-permute-start = (f32[8,16,64]{2,1,0:T(8,128)S(1)}, f32[8,16,64]{2,1,0:T(8,128)S(1)}, u32[]{:S(2)}, u32[]{:S(2)}) collective-permute-start(f32[8,16,64]{2,1,0:T(8,128)S(1)} %get-tuple-element.1044), channel_id=1, source_target_pairs={{0,8},{8,16},{16,24},{24,0},{1,9},{9,17},{17,25},{25,1},{2,10},{10... | collective-permute-start | bytes 98312 | tf_op jit(solution)/shard_map/while/body/eval_jaxpr/ppermute | solution.py:30
  71.5 14.1 %collective-permute-start = (f32[8,16,64]{2,1,0:T(8,128)S(1)}, f32[8,16,64]{2,1,0:T(8,128)S(1)}, u32[]{:S(2)}, u32[]{:S(2)}) collective-permute-start(f32[8,16,64]{2,1,0:T(8,128)S(1)} %get-tuple-element.1044), channel_id=1, source_target_pairs={{0,8},{8,16},{16,24},{24,0},{1,9},{9,17},{17,25},{25,1},{2,10},{10... | collective-permute-start | bytes 98312 | tf_op jit(solution)/shard_map/while/body/eval_jaxpr/ppermute | solution.py:30
  85.7 6.1 %collective-permute-start = (f32[8,16,64]{2,1,0:T(8,128)S(1)}, f32[8,16,64]{2,1,0:T(8,128)S(1)}, u32[]{:S(2)}, u32[]{:S(2)}) collective-permute-start(f32[8,16,64]{2,1,0:T(8,128)S(1)} %get-tuple-element.1044), channel_id=1, source_target_pairs={{0,8},{8,16},{16,24},{24,0},{1,9},{9,17},{17,25},{25,1},{2,10},{10... | collective-permute-start | bytes 98312 | tf_op jit(solution)/shard_map/while/body/eval_jaxpr/ppermute | solution.py:30
  91.9 29.0 %collective-permute-start = (f32[8,16,64]{2,1,0:T(8,128)S(1)}, f32[8,16,64]{2,1,0:T(8,128)S(1)}, u32[]{:S(2)}, u32[]{:S(2)}) collective-permute-start(f32[8,16,64]{2,1,0:T(8,128)S(1)} %get-tuple-element.1044), channel_id=1, source_target_pairs={{0,8},{8,16},{16,24},{24,0},{1,9},{9,17},{17,25},{25,1},{2,10},{10... | collective-permute-start | bytes 98312 | tf_op jit(solution)/shard_map/while/body/eval_jaxpr/ppermute | solution.py:30
  121.0 2.0 copy-start.3
  123.0 5.7 copy-start.2
  123.0 5.1 collective-permute-start.3
  124.5 3.9 collective-permute-start.4
  134.2 5.4 collective-permute-start.5
  135.5 5.0 collective-permute-start.6
  160.8 4.3 collective-permute-start.7
  162.1 3.9 collective-permute-start.8
  191.3 4.3 collective-permute-start.9
  192.6 3.9 collective-permute-start.10
  202.3 5.7 collective-permute-start.11
  203.6 5.3 collective-permute-start.12
  231.1 4.4 collective-permute-start.13
  232.4 3.9 collective-permute-start.14
  265.8 84.9 %collective-permute-start.15 = (f32[4,64,256]{2,1,0:T(8,128)}, f32[4,64,256]{2,1,0:T(8,128)S(1)}, u32[]{:S(2)}, u32[]{:S(2)}) collective-permute-start(f32[4,64,256]{2,1,0:T(8,128)} %broadcast_subtract_fusion.1), channel_id=1, source_target_pairs={{0,8},{8,16},{16,24},{24,0},{1,9},{9,17},{17,25},{25,1},{2,10},{10... | collective-permute-start | bytes 786440 | tf_op jit(solution)/shard_map/ppermute | solution.py:30
  290.8 6.2 %collective-permute-start.1 = (f32[8,16,64]{2,1,0:T(8,128)S(1)}, f32[8,16,64]{2,1,0:T(8,128)S(1)}, u32[]{:S(2)}, u32[]{:S(2)}) collective-permute-start(f32[8,16,64]{2,1,0:T(8,128)S(1)} %get-tuple-element.929), channel_id=1, source_target_pairs={{0,8},{8,16},{16,24},{24,0},{1,9},{9,17},{17,25},{25,1},{2,10},{10... | collective-permute-start | bytes 98312 | tf_op jit(solution)/shard_map/while/body/eval_jaxpr/ppermute | solution.py:30
  297.2 14.8 %collective-permute-start.1 = (f32[8,16,64]{2,1,0:T(8,128)S(1)}, f32[8,16,64]{2,1,0:T(8,128)S(1)}, u32[]{:S(2)}, u32[]{:S(2)}) collective-permute-start(f32[8,16,64]{2,1,0:T(8,128)S(1)} %get-tuple-element.929), channel_id=1, source_target_pairs={{0,8},{8,16},{16,24},{24,0},{1,9},{9,17},{17,25},{25,1},{2,10},{10... | collective-permute-start | bytes 98312 | tf_op jit(solution)/shard_map/while/body/eval_jaxpr/ppermute | solution.py:30
  312.1 6.1 %collective-permute-start.1 = (f32[8,16,64]{2,1,0:T(8,128)S(1)}, f32[8,16,64]{2,1,0:T(8,128)S(1)}, u32[]{:S(2)}, u32[]{:S(2)}) collective-permute-start(f32[8,16,64]{2,1,0:T(8,128)S(1)} %get-tuple-element.929), channel_id=1, source_target_pairs={{0,8},{8,16},{16,24},{24,0},{1,9},{9,17},{17,25},{25,1},{2,10},{10... | collective-permute-start | bytes 98312 | tf_op jit(solution)/shard_map/while/body/eval_jaxpr/ppermute | solution.py:30
  318.3 30.4 %collective-permute-start.1 = (f32[8,16,64]{2,1,0:T(8,128)S(1)}, f32[8,16,64]{2,1,0:T(8,128)S(1)}, u32[]{:S(2)}, u32[]{:S(2)}) collective-permute-start(f32[8,16,64]{2,1,0:T(8,128)S(1)} %get-tuple-element.929), channel_id=1, source_target_pairs={{0,8},{8,16},{16,24},{24,0},{1,9},{9,17},{17,25},{25,1},{2,10},{10... | collective-permute-start | bytes 98312 | tf_op jit(solution)/shard_map/while/body/eval_jaxpr/ppermute | solution.py:30
  349.1 7.2 %copy-start.5 = (f32[1,4,64,256]{3,2,1,0:T(8,128)S(1)}, f32[1,4,64,256]{3,2,1,0:T(8,128)}, u32[]{:S(2)}) copy-start(f32[1,4,64,256]{3,2,1,0:T(8,128)} %get-tuple-element.743) | copy-start | bytes 786436
  350.8 4.3 collective-permute-start.16
  352.1 3.9 collective-permute-start.17
  359.2 4.3 collective-permute-start.18
  360.5 3.9 collective-permute-start.19
  385.8 4.3 collective-permute-start.20
  387.1 3.9 collective-permute-start.21
  391.3 29.2 %copy-start.6 = (f32[1,4,64,256]{3,2,1,0:T(8,128)S(1)}, f32[1,4,64,256]{3,2,1,0:T(8,128)}, u32[]{:S(2)}) copy-start(f32[1,4,64,256]{3,2,1,0:T(8,128)} %get-tuple-element.740) | copy-start | bytes 786436
  415.0 4.3 collective-permute-start.22
  416.3 3.9 collective-permute-start.23
  423.4 5.7 collective-permute-start.24
  424.7 5.3 collective-permute-start.25
  452.2 4.6 collective-permute-start.26
  453.5 3.9 collective-permute-start.27
  481.9 4.4 copy-start.4
  486.3 82.3 %collective-permute-start.28 = (f32[4,64,256]{2,1,0:T(8,128)S(1)}, f32[4,64,256]{2,1,0:T(8,128)S(1)}, u32[]{:S(2)}, u32[]{:S(2)}) collective-permute-start(f32[4,64,256]{2,1,0:T(8,128)S(1)} %broadcast_subtract_fusion), channel_id=1, source_target_pairs={{0,8},{8,16},{16,24},{24,0},{1,9},{9,17},{17,25},{25,1},{2,10},{10... | collective-permute-start | bytes 786440 | tf_op jit(solution)/shard_map/ppermute | solution.py:30
  510.7 6.2 %collective-permute-start.2 = (f32[8,16,64]{2,1,0:T(8,128)S(1)}, f32[8,16,64]{2,1,0:T(8,128)S(1)}, u32[]{:S(2)}, u32[]{:S(2)}) collective-permute-start(f32[8,16,64]{2,1,0:T(8,128)S(1)} %add.2463), channel_id=1, source_target_pairs={{0,8},{8,16},{16,24},{24,0},{1,9},{9,17},{17,25},{25,1},{2,10},{10... | collective-permute-start | bytes 98312 | tf_op jit(solution)/shard_map/while/body/eval_jaxpr/ppermute | solution.py:30
  517.0 14.1 %collective-permute-start.2 = (f32[8,16,64]{2,1,0:T(8,128)S(1)}, f32[8,16,64]{2,1,0:T(8,128)S(1)}, u32[]{:S(2)}, u32[]{:S(2)}) collective-permute-start(f32[8,16,64]{2,1,0:T(8,128)S(1)} %add.2463), channel_id=1, source_target_pairs={{0,8},{8,16},{16,24},{24,0},{1,9},{9,17},{17,25},{25,1},{2,10},{10... | collective-permute-start | bytes 98312 | tf_op jit(solution)/shard_map/while/body/eval_jaxpr/ppermute | solution.py:30
  531.3 6.1 %collective-permute-start.2 = (f32[8,16,64]{2,1,0:T(8,128)S(1)}, f32[8,16,64]{2,1,0:T(8,128)S(1)}, u32[]{:S(2)}, u32[]{:S(2)}) collective-permute-start(f32[8,16,64]{2,1,0:T(8,128)S(1)} %add.2463), channel_id=1, source_target_pairs={{0,8},{8,16},{16,24},{24,0},{1,9},{9,17},{17,25},{25,1},{2,10},{10... | collective-permute-start | bytes 98312 | tf_op jit(solution)/shard_map/while/body/eval_jaxpr/ppermute | solution.py:30
  537.5 29.1 %collective-permute-start.2 = (f32[8,16,64]{2,1,0:T(8,128)S(1)}, f32[8,16,64]{2,1,0:T(8,128)S(1)}, u32[]{:S(2)}, u32[]{:S(2)}) collective-permute-start(f32[8,16,64]{2,1,0:T(8,128)S(1)} %add.2463), channel_id=1, source_target_pairs={{0,8},{8,16},{16,24},{24,0},{1,9},{9,17},{17,25},{25,1},{2,10},{10... | collective-permute-start | bytes 98312 | tf_op jit(solution)/shard_map/while/body/eval_jaxpr/ppermute | solution.py:30
where the time goes:
time: 580 us; the launch traced here: 570 us
  blocking collectives  180 us (31%)
  starting transfers between devices  137 us (24%)
  waiting for transfers between devices  96.6 us (17%)
  other arithmetic  73.3 us (13%)
  local copies, waits for them, and re-layouts  30.1 us (5%)
  loops' own time  27.4 us (5%)
  between operations  25 us (4%)
    psum x8, blocking collectives, paired_sums(): lax.psum((jnp.sum(residual * residual), jnp.sum(residual * applied)), 'sp...  131 us
    ppermute x14, waiting for transfers between devices, from_behind(): return lax.ppermute(value, axis, pairs)  87.1 us
    ppermute x14, starting transfers between devices, from_behind(): return lax.ppermute(value, axis, pairs)  81.2 us
    ppermute x12, starting transfers between devices, with_halo(): before = lax.ppermute(last, axis, up)  40.4 us
    reduce_sum x8, other arithmetic, paired_sums(): jnp.sum(residual * applied)  28.2 us
    another operation x12, loops' own time, one_turn(): stepped = lax.cond(active, advance, keep_same, current)  26.8 us
    all_gather x2, blocking collectives, body(): lax.all_gather(fine_coarse - own_share(advanced), 'space', axis=0, tiled=...  21.2 us
    sub x4, other arithmetic, fine_solve(): residual = right_side - fine_operator(solution, weight)  16.8 us
  transfers between devices with their start and end apart: 38, of which 24 were waited for; matrix products, arithmetic and copies ran while one was open for 3% of the time, Pallas kernels for 0%

commit v1 on v0

v1 whole, which is shorter than its diff:
```python
import functools

import jax
import jax.numpy as jnp
from jax import lax
from jax.experimental import pallas as pl
from jax.experimental.pallas import tpu as pltpu
from jax.sharding import PartitionSpec as P

FINE_STEPS = 2
CG_COARSE = 4
PARA_ITERS = 2
MESH = pl.DeviceIdType.MESH
HIGH = lax.Precision.HIGHEST
F32 = jnp.float32


def dot(a, b):
    return lax.dot_general(
        a, b, (((1,), (0,)), ((), ())), precision=HIGH, preferred_element_type=F32
    )


def kernel(
    T, S, lx, labels, cond, coil, currents, init, starts_out, ends_out,
    cur, setup, wt, G, D, C, rf, arb, U, R, V, SRC, SIG, HL, HH, ZB, FE, send, recv,
):
    NY, NZ = init.shape[1], init.shape[2]
    px = lx // 4
    XC = S * px
    hr, hl = NY // 8, NZ // 4
    N = T * S
    n = lax.axis_index("tm")
    s = lax.axis_index("space")
    me = n * S + s
    has_lo, has_hi = s > 0, s < S - 1
    phases = coil.shape[0]

    def others(count, own, fn):
        def step(i, carry):
            fn(lax.rem(own + i, count))
            return carry

        lax.fori_loop(1, count, step, 0)

    barrier = pltpu.get_barrier_semaphore()
    others(
        N,
        me,
        lambda d: pl.semaphore_signal(
            barrier, inc=1, device_id=(d // S, lax.rem(d, S)), device_id_type=MESH
        ),
    )

    def remote(src, dst, i, dev):
        return pltpu.make_async_remote_copy(
            src_ref=src, dst_ref=dst, send_sem=send.at[i], recv_sem=recv.at[i],
            device_id=dev, device_id_type=MESH,
        )

    def wait_on(ref, sem):
        pltpu.make_async_copy(ref, ref, sem).wait()

    up_dev, down_dev = (n, s + 1), (n, s - 1)

    rowi = lax.broadcasted_iota(jnp.int32, (NY, NZ), 0)
    coli = lax.broadcasted_iota(jnp.int32, (NY, NZ), 1)
    ey = (lax.broadcasted_iota(jnp.int32, (NY // 4, NY), 1) // 4
          == lax.broadcasted_iota(jnp.int32, (NY // 4, NY), 0)).astype(F32)
    eyt = (lax.broadcasted_iota(jnp.int32, (NY, NY // 4), 0) // 4
           == lax.broadcasted_iota(jnp.int32, (NY, NY // 4), 1)).astype(F32)
    zr = lax.broadcasted_iota(jnp.int32, (NZ, 2 * hl), 0) // 4
    zc = lax.broadcasted_iota(jnp.int32, (NZ, 2 * hl), 1)
    down_lo = (zr == zc).astype(F32)
    down_hi = (zr == zc - hl).astype(F32)
    tr = lax.broadcasted_iota(jnp.int32, (2 * hl, NZ), 0)
    tc = lax.broadcasted_iota(jnp.int32, (2 * hl, NZ), 1) // 4
    up_lo = (tr == tc).astype(F32)
    up_hi = (tr - hl == tc).astype(F32)

    def restrict4(total):
        t = dot(ey, total)
        return (dot(t[:hr], down_lo) + dot(t[hr:], down_hi)) * (1.0 / 64.0)

    def prolong(c):
        t = jnp.concatenate([dot(c, up_lo), dot(c, up_hi)], axis=0)
        return dot(eyt, t)

    def beside_yz(x):
        a = jnp.where(rowi > 0, pltpu.roll(x, 1, 0), 0.0)
        b = jnp.where(rowi < NY - 1, pltpu.roll(x, NY - 1, 0), 0.0)
        c = jnp.where(coli > 0, pltpu.roll(x, 1, 1), 0.0)
        d = jnp.where(coli < NZ - 1, pltpu.roll(x, NZ - 1, 1), 0.0)
        return (a + b) + (c + d)

    for p in range(lx):
        lab = labels[p]
        sig = jnp.where(lab == 0, cond[0], 0.0)
        for region in range(1, cond.shape[0]):
            sig = jnp.where(lab == region, cond[region], sig)
        SIG[p] = sig
        for f in range(FINE_STEPS):
            src = currents[0, f, 0] * coil[0, p]
            for ph in range(1, phases):
                src = src + currents[0, f, ph] * coil[ph, p]
            SRC[f, p + 1] = src

    for b in range(px):
        def total(get):
            return (get(4 * b) + get(4 * b + 1)) + (get(4 * b + 2) + get(4 * b + 3))

        setup[s * px + b, 0] = restrict4(total(lambda p: init[p]))
        setup[s * px + b, 1] = restrict4(total(lambda p: SIG[p]))
        for ph in range(phases):
            setup[s * px + b, 2 + ph] = restrict4(total(lambda p, ph=ph: coil[ph, p]))
    row8 = lax.broadcasted_iota(jnp.int32, (8, 2 * hl), 0)
    mean = jnp.zeros((8, 2 * hl), F32)
    for ph in range(phases):
        m = currents[0, 0, ph]
        for f in range(1, FINE_STEPS):
            m = m + currents[0, f, ph]
        mean = jnp.where(row8 == ph, m / float(FINE_STEPS), mean)
    cur[n] = mean

    zero = jnp.zeros((NY, NZ), F32)

    @pl.when(jnp.logical_not(has_lo))
    def _():
        for ref, ids in ((HL, (0, 1)), (R, (0,)), (V, (0, 1)), (SRC.at[0], (0,)), (SRC.at[1], (0,))):
            for i in ids:
                ref[i] = zero

    @pl.when(jnp.logical_not(has_hi))
    def _():
        for ref, ids in (
            (HH, (0, 1, 2)), (R, (lx + 4,)), (V, (lx + 3, lx + 4)),
            (SRC.at[0], (lx + 1, lx + 2)), (SRC.at[1], (lx + 1, lx + 2)), (SIG, (lx,)),
        ):
            for i in ids:
                ref[i] = zero

    pl.semaphore_wait(barrier, N - 1)

    mine = setup.at[pl.ds(s * px, px)]
    others(S, s, lambda d: remote(mine, mine, 0, (n, d)).start())
    others(T, n, lambda d: remote(cur.at[n], cur.at[n], 1, (d, s)).start())
    c_src_up = remote(SRC.at[:, lx], SRC.at[:, 0], 2, up_dev)
    c_src_dn = remote(SRC.at[:, pl.ds(1, 2)], SRC.at[:, pl.ds(lx + 1, 2)], 3, down_dev)
    c_sig_dn = remote(SIG.at[0], SIG.at[lx], 4, down_dev)
    c_ini_up = remote(init.at[pl.ds(lx - 2, 2)], HL, 5, up_dev)
    c_ini_dn = remote(init.at[pl.ds(0, 3)], HH, 6, down_dev)
    first = n == 0
    up_copies = ((c_src_up, None),)
    down_copies = ((c_src_dn, None), (c_sig_dn, None))

    @pl.when(jnp.logical_and(first, has_hi))
    def _():
        c_ini_up.start()

    @pl.when(jnp.logical_and(first, has_lo))
    def _():
        c_ini_dn.start()

    @pl.when(has_hi)
    def _():
        c_src_up.start()

    @pl.when(has_lo)
    def _():
        c_src_dn.start()
        c_sig_dn.start()

    crow = lax.broadcasted_iota(jnp.int32, (XC, hr, 2 * hl), 1)
    ccol = lax.broadcasted_iota(jnp.int32, (XC, hr, 2 * hl), 2)
    cz = lax.rem(ccol, hl)
    zplane = jnp.zeros((1, hr, 2 * hl), F32)

    def coarse_lap(c):
        xs = jnp.concatenate([zplane, c[:-1]], 0) + jnp.concatenate([c[1:], zplane], 0)
        w = pltpu.roll(c, hl, 2)
        za = jnp.where(cz > 0, pltpu.roll(c, 1, 2), 0.0)
        zb = jnp.where(cz < hl - 1, pltpu.roll(c, 2 * hl - 1, 2), 0.0)
        ya = pltpu.roll(
            jnp.where(crow == hr - 1, jnp.where(ccol >= hl, w, 0.0), c), 1, 1)
        yb = pltpu.roll(
            jnp.where(crow == 0, jnp.where(ccol < hl, w, 0.0), c), hr - 1, 1)
        return 0.0625 * (6.0 * c - ((xs + za) + (zb + ya) + yb))

    def total3(x):
        return jnp.sum(jnp.sum(x, axis=0), keepdims=True).reshape(1, 1, 1)

    def solve(i, c):
        source = cur[i, 0:1, :][None] * setup[:, 2]
        for ph in range(1, phases):
            source = source + cur[i, ph:ph + 1, :][None] * setup[:, 2 + ph]
        weight = wt[...]
        r = source - coarse_lap(c)
        q = weight * r + coarse_lap(r)
        rr, rq = total3(r * r), total3(r * q)
        alpha = rr / rq
        d, x = r, c
        for it in range(CG_COARSE):
            x = x + alpha * d
            if it + 1 < CG_COARSE:
                r = r - alpha * q
                w = weight * r + coarse_lap(r)
                new, rw = total3(r * r), total3(r * w)
                beta = new / rr
                alpha = new / (rw - beta * new / alpha)
                d = r + beta * d
                q = w + beta * q
                rr = new
        return x

    def solve_step(i, k):
        g = solve(i, C[...])
        if k == 0:
            D[i] = g
            C[...] = g
        else:
            diff = g - G[i]
            D[i] = diff
        G[i] = g

    def next_start(i, k):
        C[...] = D[i] + rf[k - 1, pl.ds(i * XC, XC)]

    def fine_residual(f):
        def step(i, carry):
            g = s * lx + i - 1
            u = U[i + 1]
            r = SRC[f, i] - 6.0 * u + ((U[i] + U[i + 2]) + beside_yz(u))
            inside = jnp.logical_and(g >= 0, g < S * lx)
            R[i + 1] = jnp.where(inside, r, 0.0)
            return carry

        lax.fori_loop(0, lx + 3, step, 0)

        def step_v(i, carry):
            g = s * lx + i
            r = R[i + 2]
            v = (SIG[i] + 6.0) * r - ((R[i + 1] + R[i + 3]) + beside_yz(r))
            V[i + 2] = jnp.where(g < S * lx, v, 0.0)
            return carry

        lax.fori_loop(0, lx + 1, step_v, 0)

    def fold(x):
        y = x[:, :2 * hl]
        for j in range(1, NZ // (2 * hl)):
            y = y + x[:, 2 * hl * j:2 * hl * (j + 1)]
        z = y[:8]
        for j in range(1, NY // 8):
            z = z + y[8 * j:8 * (j + 1)]
        return z

    def fine_moments(stage):
        def step(i, carry):
            m0, m1, m2, m3 = carry
            r, v = R[i + 2], V[i + 2]
            link = V[i + 3] + jnp.where(rowi > 0, pltpu.roll(v, 1, 0), 0.0)
            link = link + jnp.where(coli > 0, pltpu.roll(v, 1, 1), 0.0)
            av = (SIG[i] + 6.0) * v - 2.0 * link
            return (m0 + fold(r * r), m1 + fold(r * v), m2 + fold(v * v), m3 + fold(v * av))

        z8 = jnp.zeros((8, 2 * hl), F32)
        ms = lax.fori_loop(0, lx, step, (z8, z8, z8, z8))
        block = jnp.zeros((8, 2 * hl), F32)
        for j, m in enumerate(ms):
            block = jnp.where(row8 == j, jnp.sum(m, axis=0, keepdims=True), block)
        arb[stage, s] = block
        others(
            S, s, lambda d: remote(arb.at[stage, s], arb.at[stage, s], 8 + stage, (n, d)).start()
        )

    def fine_coefficients(stage):
        wait_on(arb.at[stage, pl.ds(0, S - 1)], recv.at[8 + stage])
        m = jnp.sum(jnp.sum(arb[stage], axis=0), axis=1, keepdims=True)
        m0, m1, m2, m3 = (m[j:j + 1] for j in range(4))
        q1, q2, q3 = m1 / m0, m2 / m1, m3 / m2
        gap = q3 - q2
        plain = gap <= 1e-6 * q3
        gap = jnp.where(plain, 1.0, gap)
        a = jnp.where(plain, 1.0 / q1, (q3 - q1) / (q1 * gap))
        b = jnp.where(plain, 0.0, (q1 - q2) / (q1 * q2 * gap))
        return a, b

    def halo_copies(k):
        base = 12 + 4 * k
        ups = (
            remote(R.at[lx], R.at[0], base, up_dev),
            remote(V.at[pl.ds(lx, 2)], V.at[pl.ds(0, 2)], base + 1, up_dev),
        )
        downs = (
            remote(R.at[4], R.at[lx + 4], base + 2, down_dev),
            remote(V.at[pl.ds(3, 2)], V.at[pl.ds(lx + 3, 2)], base + 3, down_dev),
        )
        return ups, downs

    def fine_run(k):
        fine_residual(0)
        fine_moments(2 * k)
        ups, downs = halo_copies(k)

        @pl.when(has_hi)
        def _():
            for c in ups:
                c.start()

        @pl.when(has_lo)
        def _():
            for c in downs:
                c.start()

        a, b = fine_coefficients(2 * k)

        @pl.when(has_hi)
        def _():
            for c in ups:
                c.wait_send()
            for c in downs:
                c.wait_recv()

        @pl.when(has_lo)
        def _():
            for c in downs:
                c.wait_send()
            for c in ups:
                c.wait_recv()

        def update(i, carry):
            U[i] = U[i] + a * R[i] + b * V[i]
            return carry

        lax.fori_loop(0, lx + 5, update, 0)
        fine_residual(1)
        fine_moments(2 * k + 1)
        a, b = fine_coefficients(2 * k + 1)

        for p in range(lx):
            value = U[p + 2] + a * R[p + 2] + b * V[p + 2]
            FE[k, p] = value
            if k == PARA_ITERS - 1:
                ends_out[0, p] = value
        for blk in range(px):
            tot = (FE[k, 4 * blk] + FE[k, 4 * blk + 1]) + (FE[k, 4 * blk + 2] + FE[k, 4 * blk + 3])
            rf[k, me * px + blk] = restrict4(tot)
        part = rf.at[k, pl.ds(me * px, px)]
        others(N, me, lambda d: remote(part, part, 20 + k, (d // S, lax.rem(d, S))).start())

    def z_copy(k):
        return remote(FE.at[k], ZB.at[k], 22 + k, (lax.rem(n + 1, T), s))

    def rf_wait(k):
        wait_on(rf.at[k, pl.ds(0, (N - 1) * px)], recv.at[20 + k])

    wait_on(setup.at[pl.ds(0, (S - 1) * px)], recv.at[0])
    wait_on(cur.at[pl.ds(0, T - 1)], recv.at[1])
    wt[...] = setup[:, 1] / float(FINE_STEPS)
    C[...] = setup[:, 0]

    def sweep0(i, carry):
        solve_step(i, 0)
        return carry

    lax.fori_loop(0, T - 1, sweep0, 0)

    prev = lax.rem(n + T - 1, T)
    below = jnp.maximum(s * px - 1, 0)
    above = jnp.minimum(s * px + px, XC - 1)

    def put_prolonged(rest):
        lo = jnp.where(has_lo, prolong(D[prev, below]), 0.0)
        hi = jnp.where(has_hi, prolong(D[prev, above]), 0.0)
        own = [prolong(D[prev, s * px + blk]) for blk in range(px)]
        for i in range(2):
            U[i] = lo + HL[i] if rest else lo
        for i in range(lx):
            U[i + 2] = own[i // 4] + ZB[0, i] if rest else own[i // 4]
        for i in range(3):
            U[lx + 2 + i] = hi + HH[i] if rest else hi

    @pl.when(has_hi)
    def _():
        c_src_up.wait_send()
        c_src_dn.wait_recv()
        c_sig_dn.wait_recv()

    @pl.when(has_lo)
    def _():
        c_src_dn.wait_send()
        c_sig_dn.wait_send()
        c_src_up.wait_recv()

    @pl.when(first)
    def _():
        @pl.when(has_hi)
        def _():
            c_ini_up.wait_send()
            c_ini_dn.wait_recv()

        @pl.when(has_lo)
        def _():
            c_ini_dn.wait_send()
            c_ini_up.wait_recv()

        for i in range(2):
            U[i] = HL[i]
        for i in range(lx):
            U[i + 2] = init[i]
        for i in range(3):
            U[lx + 2 + i] = HH[i]

    @pl.when(jnp.logical_not(first))
    def _():
        put_prolonged(False)

    fine_run(0)
    z0 = z_copy(0)
    z0.start()

    solve_step(T - 1, 0)
    solve_step(0, 1)

    rf_wait(0)

    def sweep1(i, carry):
        next_start(i - 1, 1)
        solve_step(i, 1)
        return carry

    r_up = remote(ZB.at[0, pl.ds(lx - 2, 2)], HL, 24, up_dev)
    r_dn = remote(ZB.at[0, pl.ds(0, 3)], HH, 25, down_dev)
    later = jnp.logical_not(first)

    @pl.when(later)
    def _():
        z0.wait_recv()

        @pl.when(has_hi)
        def _():
            r_up.start()

        @pl.when(has_lo)
        def _():
            r_dn.start()

    lax.fori_loop(1, T - 1, sweep1, 0)

    @pl.when(later)
    def _():
        @pl.when(has_hi)
        def _():
            r_up.wait_send()
            r_dn.wait_recv()

        @pl.when(has_lo)
        def _():
            r_dn.wait_send()
            r_up.wait_recv()

        put_prolonged(True)

    @pl.when(first)
    def _():
        put_prolonged(False)

    fine_run(1)
    z1 = z_copy(1)

    @pl.when(n < T - 1)
    def _():
        z1.start()

    next_start(T - 2, 1)
    solve_step(T - 1, 1)
    next_start(T - 1, 1)
    solve_step(0, 2)
    rf_wait(1)

    def sweep2(i, carry):
        next_start(i - 1, 2)
        solve_step(i, 2)
        return carry

    lax.fori_loop(1, T - 1, sweep2, 0)

    @pl.when(first)
    def _():
        z0.wait_recv()

    @pl.when(later)
    def _():
        z1.wait_recv()

    slot = jnp.minimum(n, 1)
    for i in range(lx):
        starts_out[0, i] = ZB[slot, i] + prolong(D[prev, s * px + i // 4])

    z0.wait_send()

    @pl.when(n < T - 1)
    def _():
        z1.wait_send()

    wait_on(setup.at[pl.ds(0, (S - 1) * px)], send.at[0])
    wait_on(cur.at[pl.ds(0, T - 1)], send.at[1])
    for stage in range(2 * PARA_ITERS):
        wait_on(arb.at[stage, pl.ds(0, S - 1)], send.at[8 + stage])
    for k in range(PARA_ITERS):
        wait_on(rf.at[k, pl.ds(0, (N - 1) * px)], send.at[20 + k])


def body(T, S, labels, conductivity, coil_pattern, currents, initial_state):
    lx, NY, NZ = initial_state.shape
    phases = coil_pattern.shape[0]
    px = lx // 4
    XC = S * px
    hr, hl = NY // 8, NZ // 4
    vm = pl.BlockSpec(memory_space=pltpu.VMEM)
    sm = pl.BlockSpec(memory_space=pltpu.SMEM)
    shape = jax.ShapeDtypeStruct((1, lx, NY, NZ), F32)
    coarse = (XC, hr, 2 * hl)

    def plane(*lead):
        return pltpu.VMEM(lead + (NY, NZ), F32)

    return pl.pallas_call(
        functools.partial(kernel, T, S, lx),
        out_shape=(shape, shape),
        in_specs=[vm, sm, vm, sm, vm],
        out_specs=(vm, vm),
        scratch_shapes=[
            pltpu.VMEM((T, 8, 2 * hl), F32),
            pltpu.VMEM((XC, 2 + phases, hr, 2 * hl), F32),
            pltpu.VMEM(coarse, F32),
            pltpu.VMEM((T,) + coarse, F32),
            pltpu.VMEM((T,) + coarse, F32),
            pltpu.VMEM(coarse, F32),
            pltpu.VMEM((PARA_ITERS, T * XC) + coarse[1:], F32),
            pltpu.VMEM((2 * PARA_ITERS, S, 8, 2 * hl), F32),
            plane(lx + 5),
            plane(lx + 5),
            plane(lx + 5),
            plane(FINE_STEPS, lx + 3),
            plane(lx + 1),
            plane(2),
            plane(3),
            plane(PARA_ITERS, lx),
            plane(PARA_ITERS, lx),
            pltpu.SemaphoreType.DMA((26,)),
            pltpu.SemaphoreType.DMA((26,)),
        ],
        compiler_params=pltpu.CompilerParams(
            collective_id=0, has_side_effects=True, vmem_limit_bytes=56 * 1024 * 1024
        ),
    )(labels, conductivity, coil_pattern, currents, initial_state)


def solution(mesh):
    T, S = mesh.shape["tm"], mesh.shape["space"]
    in_specs = (
        P("space", None, None),
        P(),
        P(None, "space", None, None),
        P("tm", None, None),
        P("space", None, None),
    )
    out_specs = (P("tm", "space", None, None), P("tm", "space", None, None))
    return jax.shard_map(
        functools.partial(body, T, S), mesh=mesh, in_specs=in_specs, out_specs=out_specs,
        check_vma=False,
    )
```

time: 580 us -> 75.3 us (0.13); the launches traced: 570 us -> 74.5 us
  blocking collectives: 180 us -> 0 us
  starting transfers between devices: 137 us -> 0 us
  waiting for transfers between devices: 96.6 us -> 0 us
  other arithmetic: 73.3 us -> 0 us
  Pallas kernels: 0 us -> 71.4 us
  local copies, waits for them, and re-layouts: 30.1 us -> 2.42 us
  loops' own time: 27.4 us -> 0 us
  between operations: 25 us -> 0.65 us
    ppermute x38 -> x0, starting transfers between devices: 137 us -> none  [the longest x14 81.2 us: from_behind(): return lax.ppermute(value, axis, pairs)]
    psum x8 -> x0, blocking collectives: 131 us -> none  [paired_sums(): lax.psum((jnp.sum(residual * residual), jnp.sum(residual * applied)), 'sp...]
    ppermute x38 -> x0, waiting for transfers between devices: 96.6 us -> none  [the longest x14 87.1 us: from_behind(): return lax.ppermute(value, axis, pairs)]
    pallas_call x0 -> x1, Pallas kernels: none -> 71.4 us  [body(): pl.pallas_call(functools.partial(kernel, T, S, lx), out_shape=(shape, sha...]
    all_gather x5 -> x0, blocking collectives: 49.7 us -> none  [the longest x2 21.2 us: body(): lax.all_gather(fine_coarse - own_share(advanced), 'space', axis=0, tiled=...]
    reduce_sum x42 -> x0, other arithmetic: 48.7 us -> none  [the longest x8 28.2 us: paired_sums(): jnp.sum(residual * applied)]
    another operation x15 -> x0, loops' own time: 27.4 us -> none  [the longest x12 26.8 us: one_turn(): stepped = lax.cond(active, advance, keep_same, current)]
    sub x15 -> x0, other arithmetic: 18 us -> none  [the longest x4 16.8 us: fine_solve(): residual = right_side - fine_operator(solution, weight)]
  transfers between devices with their start and end apart: 38 -> 0, of which waited for: 24 -> 0; matrix products, arithmetic and copies ran while one was open for 3% -> 0% of each run, Pallas kernels for 0% -> 0%
where the time goes in v1:
time: 75.3 us; the launch traced here: 74.5 us
  Pallas kernels  71.4 us (95%)
  local copies, waits for them, and re-layouts  2.42 us (3%)
    pallas_call x1, Pallas kernels, body(): pl.pallas_call(functools.partial(kernel, T, S, lx), out_shape=(shape, sha...  71.4 us
    unnamed x4, local copies, waits for them, and re-layouts  2.42 us

profile of v1, /device:TPU:0, one launch (start us, length us, event | category | flops | bytes accessed | tf_op | source)
XLA Modules:
  0.0 74.5 jit_solution(15631833296862090743)
XLA Ops:
  0.6 71.4 %shard_map.68 = (f32[1,4,64,256]{3,2,1,0:T(8,128)}, f32[1,4,64,256]{3,2,1,0:T(8,128)}) custom-call(s32[4,64,256]{2,1,0:T(8,128)} %labels.1, f32[4]{0:T(128)} %cond.1, f32[3,4,64,256]{3,2,1,0:T(8,128)} %coil.1, f32[1,2,3]{2,1,0:T(2,128)} %currents.1, f32[4,64,256]{2,1,0:T(8,128)} %init.1), custom_call_target="tpu_custom_call" | custom-call | tf_op jit(solution)/shard_map/pallas_call | solution.py:528
  72.1 0.0 copy-start
  72.1 1.7 %copy.9 = f32[1,4,64,256]{3,2,1,0:T(8,128)} copy(f32[1,4,64,256]{3,2,1,0:T(8,128)} %get-tuple-element.4) | data formatting | bytes 524288
  73.8 0.0 copy-done
  73.8 0.7 copy.10
Async XLA Ops:
  72.1 1.7 %copy-start = (f32[1,4,64,256]{3,2,1,0:T(8,128)S(1)}, f32[1,4,64,256]{3,2,1,0:T(8,128)}, u32[]{:S(2)}) copy-start(f32[1,4,64,256]{3,2,1,0:T(8,128)} %get-tuple-element.5) | copy-start | bytes 786436

commit v2 on v1

--- a/solution.py
+++ b/solution.py
@@ -22,10 +22,18 @@
 
 
 def kernel(
-    T, S, lx, labels, cond, coil, currents, init, starts_out, ends_out,
-    cur, setup, wt, G, D, C, rf, arb, U, R, V, SRC, SIG, HL, HH, ZB, FE, send, recv,
+    T, S, lx, labels_in, cond, coil_in, currents, init_in, starts_out, ends_out,
+    cur, setup, wt, G, D, C, rf, arb, U, R, V, coil, labels, init, SIG, HL, HH, ZB, FE,
+    send, recv, load,
 ):
     NY, NZ = init.shape[1], init.shape[2]
+    loads = [
+        pltpu.make_async_copy(init_in, init, load.at[0]),
+        pltpu.make_async_copy(labels_in, labels, load.at[1]),
+        pltpu.make_async_copy(coil_in, coil.at[:, pl.ds(1, lx)], load.at[2]),
+    ]
+    for c in loads:
+        c.start()
     px = lx // 4
     XC = S * px
     hr, hl = NY // 8, NZ // 4
@@ -36,20 +44,27 @@
     has_lo, has_hi = s > 0, s < S - 1
     phases = coil.shape[0]
 
+    prev = lax.rem(n + T - 1, T)
+
     def others(count, own, fn):
-        def step(i, carry):
+        for i in range(1, count):
             fn(lax.rem(own + i, count))
+
+    def everyone(fn):
+        def step(j, carry):
+            dn = lax.rem(n + j, T)
+            for i in range(S):
+                fn(dn, lax.rem(s + i, S))
             return carry
 
-        lax.fori_loop(1, count, step, 0)
+        lax.fori_loop(1, T, step, 0)
+        others(S, s, lambda d: fn(n, d))
 
     barrier = pltpu.get_barrier_semaphore()
-    others(
-        N,
-        me,
-        lambda d: pl.semaphore_signal(
-            barrier, inc=1, device_id=(d // S, lax.rem(d, S)), device_id_type=MESH
-        ),
+    everyone(
+        lambda dn, d: pl.semaphore_signal(
+            barrier, inc=1, device_id=(dn, d), device_id_type=MESH
+        )
     )
 
     def remote(src, dst, i, dev):
@@ -93,17 +108,14 @@
         d = jnp.where(coli < NZ - 1, pltpu.roll(x, NZ - 1, 1), 0.0)
         return (a + b) + (c + d)
 
+    for c in loads:
+        c.wait()
     for p in range(lx):
         lab = labels[p]
         sig = jnp.where(lab == 0, cond[0], 0.0)
         for region in range(1, cond.shape[0]):
             sig = jnp.where(lab == region, cond[region], sig)
         SIG[p] = sig
-        for f in range(FINE_STEPS):
-            src = currents[0, f, 0] * coil[0, p]
-            for ph in range(1, phases):
-                src = src + currents[0, f, ph] * coil[ph, p]
-            SRC[f, p + 1] = src
 
     for b in range(px):
         def total(get):
@@ -112,46 +124,52 @@
         setup[s * px + b, 0] = restrict4(total(lambda p: init[p]))
         setup[s * px + b, 1] = restrict4(total(lambda p: SIG[p]))
         for ph in range(phases):
-            setup[s * px + b, 2 + ph] = restrict4(total(lambda p, ph=ph: coil[ph, p]))
+            setup[s * px + b, 2 + ph] = restrict4(total(lambda p, ph=ph: coil[ph, p + 1]))
     row8 = lax.broadcasted_iota(jnp.int32, (8, 2 * hl), 0)
-    mean = jnp.zeros((8, 2 * hl), F32)
+    row16 = lax.broadcasted_iota(jnp.int32, (16, 2 * hl), 0)
+    rows = jnp.zeros((16, 2 * hl), F32)
     for ph in range(phases):
         m = currents[0, 0, ph]
         for f in range(1, FINE_STEPS):
             m = m + currents[0, f, ph]
-        mean = jnp.where(row8 == ph, m / float(FINE_STEPS), mean)
-    cur[n] = mean
+        rows = jnp.where(row16 == ph, m / float(FINE_STEPS), rows)
+        for f in range(FINE_STEPS):
+            rows = jnp.where(row16 == phases * (1 + f) + ph, currents[0, f, ph], rows)
+    cur[n] = rows
 
     zero = jnp.zeros((NY, NZ), F32)
 
     @pl.when(jnp.logical_not(has_lo))
     def _():
-        for ref, ids in ((HL, (0, 1)), (R, (0,)), (V, (0, 1)), (SRC.at[0], (0,)), (SRC.at[1], (0,))):
+        for ref, ids in ((HL.at[0], (0, 1)), (HL.at[1], (0, 1)), (R, (0,)), (V, (0, 1))):
             for i in ids:
                 ref[i] = zero
+        for ph in range(phases):
+            coil[ph, 0] = zero
 
     @pl.when(jnp.logical_not(has_hi))
     def _():
         for ref, ids in (
-            (HH, (0, 1, 2)), (R, (lx + 4,)), (V, (lx + 3, lx + 4)),
-            (SRC.at[0], (lx + 1, lx + 2)), (SRC.at[1], (lx + 1, lx + 2)), (SIG, (lx,)),
+            (HH.at[0], (0, 1, 2)), (HH.at[1], (0, 1, 2)),
+            (R, (lx + 4,)), (V, (lx + 3, lx + 4)), (SIG, (lx,)),
         ):
             for i in ids:
                 ref[i] = zero
+        for ph in range(phases):
+            coil[ph, lx + 1] = zero
+            coil[ph, lx + 2] = zero
 
     pl.semaphore_wait(barrier, N - 1)
 
     mine = setup.at[pl.ds(s * px, px)]
+    others(T, n, lambda d: remote(cur.at[n], cur.at[n], 1, (d, s)).start())
     others(S, s, lambda d: remote(mine, mine, 0, (n, d)).start())
-    others(T, n, lambda d: remote(cur.at[n], cur.at[n], 1, (d, s)).start())
-    c_src_up = remote(SRC.at[:, lx], SRC.at[:, 0], 2, up_dev)
-    c_src_dn = remote(SRC.at[:, pl.ds(1, 2)], SRC.at[:, pl.ds(lx + 1, 2)], 3, down_dev)
+    c_src_up = remote(coil.at[:, lx], coil.at[:, 0], 2, up_dev)
+    c_src_dn = remote(coil.at[:, pl.ds(1, 2)], coil.at[:, pl.ds(lx + 1, 2)], 3, down_dev)
     c_sig_dn = remote(SIG.at[0], SIG.at[lx], 4, down_dev)
-    c_ini_up = remote(init.at[pl.ds(lx - 2, 2)], HL, 5, up_dev)
-    c_ini_dn = remote(init.at[pl.ds(0, 3)], HH, 6, down_dev)
-    first = n == 0
-    up_copies = ((c_src_up, None),)
-    down_copies = ((c_src_dn, None), (c_sig_dn, None))
+    c_ini_up = remote(init.at[pl.ds(lx - 2, 2)], HL.at[0], 5, up_dev)
+    c_ini_dn = remote(init.at[pl.ds(0, 3)], HH.at[0], 6, down_dev)
+    first = prev == 0
 
     @pl.when(jnp.logical_and(first, has_hi))
     def _():
@@ -225,11 +243,18 @@
     def next_start(i, k):
         C[...] = D[i] + rf[k - 1, pl.ds(i * XC, XC)]
 
-    def fine_residual(f):
+    def fine_residual(f, sl):
+        amps = [
+            cur[sl, phases * (1 + f) + ph:phases * (1 + f) + ph + 1, 0:1] for ph in range(phases)
+        ]
+
         def step(i, carry):
             g = s * lx + i - 1
             u = U[i + 1]
-            r = SRC[f, i] - 6.0 * u + ((U[i] + U[i + 2]) + beside_yz(u))
+            source = amps[0] * coil[0, i]
+            for ph in range(1, phases):
+                source = source + amps[ph] * coil[ph, i]
+            r = source - 6.0 * u + ((U[i] + U[i + 2]) + beside_yz(u))
             inside = jnp.logical_and(g >= 0, g < S * lx)
             R[i + 1] = jnp.where(inside, r, 0.0)
             return carry
@@ -297,8 +322,8 @@
         )
         return ups, downs
 
-    def fine_run(k):
-        fine_residual(0)
+    def fine_run(k, sl):
+        fine_residual(0, sl)
         fine_moments(2 * k)
         ups, downs = halo_copies(k)
 
@@ -333,23 +358,18 @@
             return carry
 
         lax.fori_loop(0, lx + 5, update, 0)
-        fine_residual(1)
+        fine_residual(1, sl)
         fine_moments(2 * k + 1)
         a, b = fine_coefficients(2 * k + 1)
 
         for p in range(lx):
             value = U[p + 2] + a * R[p + 2] + b * V[p + 2]
             FE[k, p] = value
-            if k == PARA_ITERS - 1:
-                ends_out[0, p] = value
         for blk in range(px):
             tot = (FE[k, 4 * blk] + FE[k, 4 * blk + 1]) + (FE[k, 4 * blk + 2] + FE[k, 4 * blk + 3])
-            rf[k, me * px + blk] = restrict4(tot)
-        part = rf.at[k, pl.ds(me * px, px)]
-        others(N, me, lambda d: remote(part, part, 20 + k, (d // S, lax.rem(d, S))).start())
-
-    def z_copy(k):
-        return remote(FE.at[k], ZB.at[k], 22 + k, (lax.rem(n + 1, T), s))
+            rf[k, (sl * S + s) * px + blk] = restrict4(tot)
+        part = rf.at[k, pl.ds((sl * S + s) * px, px)]
+        everyone(lambda dn, d: remote(part, part, 20 + k, (dn, d)).start())
 
     def rf_wait(k):
         wait_on(rf.at[k, pl.ds(0, (N - 1) * px)], recv.at[20 + k])
@@ -365,20 +385,19 @@
 
     lax.fori_loop(0, T - 1, sweep0, 0)
 
-    prev = lax.rem(n + T - 1, T)
     below = jnp.maximum(s * px - 1, 0)
     above = jnp.minimum(s * px + px, XC - 1)
 
-    def put_prolonged(rest):
-        lo = jnp.where(has_lo, prolong(D[prev, below]), 0.0)
-        hi = jnp.where(has_hi, prolong(D[prev, above]), 0.0)
-        own = [prolong(D[prev, s * px + blk]) for blk in range(px)]
+    def put_prolonged(at, rest):
+        lo = jnp.where(has_lo, prolong(D[at, below]), 0.0)
+        hi = jnp.where(has_hi, prolong(D[at, above]), 0.0)
+        own = [prolong(D[at, s * px + blk]) for blk in range(px)]
         for i in range(2):
-            U[i] = lo + HL[i] if rest else lo
+            U[i] = lo + HL[1, i] if rest else lo
         for i in range(lx):
-            U[i + 2] = own[i // 4] + ZB[0, i] if rest else own[i // 4]
+            U[i + 2] = own[i // 4] + FE[0, i] if rest else own[i // 4]
         for i in range(3):
-            U[lx + 2 + i] = hi + HH[i] if rest else hi
+            U[lx + 2 + i] = hi + HH[1, i] if rest else hi
 
     @pl.when(has_hi)
     def _():
@@ -405,19 +424,28 @@
             c_ini_up.wait_recv()
 
         for i in range(2):
-            U[i] = HL[i]
+            U[i] = HL[0, i]
         for i in range(lx):
             U[i + 2] = init[i]
         for i in range(3):
-            U[lx + 2 + i] = HH[i]
+            U[lx + 2 + i] = HH[0, i]
 
     @pl.when(jnp.logical_not(first))
     def _():
-        put_prolonged(False)
-
-    fine_run(0)
-    z0 = z_copy(0)
-    z0.start()
+        put_prolonged(lax.rem(n + T - 2, T), False)
+
+    fine_run(0, prev)
+    later = n > 0
+    r_up = remote(FE.at[0, pl.ds(lx - 2, 2)], HL.at[1], 24, up_dev)
+    r_dn = remote(FE.at[0, pl.ds(0, 3)], HH.at[1], 25, down_dev)
+
+    @pl.when(jnp.logical_and(later, has_hi))
+    def _():
+        r_up.start()
+
+    @pl.when(jnp.logical_and(later, has_lo))
+    def _():
+        r_dn.start()
 
     solve_step(T - 1, 0)
     solve_step(0, 1)
@@ -429,22 +457,6 @@
         solve_step(i, 1)
         return carry
 
-    r_up = remote(ZB.at[0, pl.ds(lx - 2, 2)], HL, 24, up_dev)
-    r_dn = remote(ZB.at[0, pl.ds(0, 3)], HH, 25, down_dev)
-    later = jnp.logical_not(first)
-
-    @pl.when(later)
-    def _():
-        z0.wait_recv()
-
-        @pl.when(has_hi)
-        def _():
-            r_up.start()
-
-        @pl.when(has_lo)
-        def _():
-            r_dn.start()
-
     lax.fori_loop(1, T - 1, sweep1, 0)
 
     @pl.when(later)
@@ -459,14 +471,16 @@
             r_dn.wait_send()
             r_up.wait_recv()
 
-        put_prolonged(True)
-
-    @pl.when(first)
-    def _():
-        put_prolonged(False)
-
-    fine_run(1)
-    z1 = z_copy(1)
+        put_prolonged(prev, True)
+
+    @pl.when(jnp.logical_not(later))
+    def _():
+        put_prolonged(prev, False)
+
+    fine_run(1, n)
+    z1 = remote(FE.at[1], ZB, 22, (lax.rem(n + 1, T), s))
+    put_ends = pltpu.make_async_copy(FE.at[1], ends_out.at[0], load.at[0])
+    put_ends.start()
 
     @pl.when(n < T - 1)
     def _():
@@ -485,19 +499,19 @@
 
     lax.fori_loop(1, T - 1, sweep2, 0)
 
-    @pl.when(first)
-    def _():
-        z0.wait_recv()
-
     @pl.when(later)
     def _():
         z1.wait_recv()
-
-    slot = jnp.minimum(n, 1)
-    for i in range(lx):
-        starts_out[0, i] = ZB[slot, i] + prolong(D[prev, s * px + i // 4])
-
-    z0.wait_send()
+        for i in range(lx):
+            U[i] = ZB[i] + prolong(D[prev, s * px + i // 4])
+
+    @pl.when(jnp.logical_not(later))
+    def _():
+        for i in range(lx):
+            U[i] = FE[0, i] + prolong(D[prev, s * px + i // 4])
+
+    put_starts = pltpu.make_async_copy(U.at[pl.ds(0, lx)], starts_out.at[0], load.at[1])
+    put_starts.start()
 
     @pl.when(n < T - 1)
     def _():
@@ -509,6 +523,8 @@
         wait_on(arb.at[stage, pl.ds(0, S - 1)], send.at[8 + stage])
     for k in range(PARA_ITERS):
         wait_on(rf.at[k, pl.ds(0, (N - 1) * px)], send.at[20 + k])
+    put_ends.wait()
+    put_starts.wait()
 
 
 def body(T, S, labels, conductivity, coil_pattern, currents, initial_state):
@@ -517,7 +533,7 @@
     px = lx // 4
     XC = S * px
     hr, hl = NY // 8, NZ // 4
-    vm = pl.BlockSpec(memory_space=pltpu.VMEM)
+    hb = pl.BlockSpec(memory_space=pl.ANY)
     sm = pl.BlockSpec(memory_space=pltpu.SMEM)
     shape = jax.ShapeDtypeStruct((1, lx, NY, NZ), F32)
     coarse = (XC, hr, 2 * hl)
@@ -528,10 +544,10 @@
     return pl.pallas_call(
         functools.partial(kernel, T, S, lx),
         out_shape=(shape, shape),
-        in_specs=[vm, sm, vm, sm, vm],
-        out_specs=(vm, vm),
+        in_specs=[hb, sm, hb, sm, hb],
+        out_specs=(hb, hb),
         scratch_shapes=[
-            pltpu.VMEM((T, 8, 2 * hl), F32),
+            pltpu.VMEM((T, 16, 2 * hl), F32),
             pltpu.VMEM((XC, 2 + phases, hr, 2 * hl), F32),
             pltpu.VMEM(coarse, F32),
             pltpu.VMEM((T,) + coarse, F32),
@@ -542,14 +558,17 @@
             plane(lx + 5),
             plane(lx + 5),
             plane(lx + 5),
-            plane(FINE_STEPS, lx + 3),
+            plane(phases, lx + 3),
+            pltpu.VMEM((lx, NY, NZ), labels.dtype),
+            plane(lx),
             plane(lx + 1),
-            plane(2),
-            plane(3),
-            plane(PARA_ITERS, lx),
+            plane(2, 2),
+            plane(2, 3),
+            plane(lx),
             plane(PARA_ITERS, lx),
             pltpu.SemaphoreType.DMA((26,)),
             pltpu.SemaphoreType.DMA((26,)),
+            pltpu.SemaphoreType.DMA((3,)),
         ],
         compiler_params=pltpu.CompilerParams(
             collective_id=0, has_side_effects=True, vmem_limit_bytes=56 * 1024 * 1024

time: 75.3 us -> 68.9 us (0.915)
  Pallas kernels: 71.4 us -> 65.6 us
    pallas_call x1, Pallas kernels: 71.4 us -> 65.6 us  [body(): pl.pallas_call(functools.partial(kernel, T, S, lx), out_shape=(shape, sha...]
where the time goes in v2:
time: 68.9 us; the launch traced here: 68.7 us
  Pallas kernels  65.6 us (95%)
  local copies, waits for them, and re-layouts  2.42 us (4%)
    pallas_call x1, Pallas kernels, body(): pl.pallas_call(functools.partial(kernel, T, S, lx), out_shape=(shape, sha...  65.6 us
    unnamed x4, local copies, waits for them, and re-layouts  2.42 us

profile of v2, /device:TPU:0, one launch (start us, length us, event | category | flops | bytes accessed | tf_op | source)
XLA Modules:
  0.0 68.7 jit_solution(8505281014952941531)
XLA Ops:
  0.6 65.6 %shard_map.68 = (f32[1,4,64,256]{3,2,1,0:T(8,128)}, f32[1,4,64,256]{3,2,1,0:T(8,128)}) custom-call(s32[4,64,256]{2,1,0:T(8,128)} %labels_in.1, f32[4]{0:T(128)} %cond.1, f32[3,4,64,256]{3,2,1,0:T(8,128)} %coil_in.1, f32[1,2,3]{2,1,0:T(2,128)} %currents.1, f32[4,64,256]{2,1,0:T(8,128)} %init_in.1), custom_call_target="tpu_custom_call" | custom-call | tf_op jit(solution)/shard_map/pallas_call | solution.py:544
  66.3 0.0 copy-start
  66.3 1.7 %copy.9 = f32[1,4,64,256]{3,2,1,0:T(8,128)} copy(f32[1,4,64,256]{3,2,1,0:T(8,128)} %get-tuple-element.4) | data formatting | bytes 524288
  68.0 0.0 copy-done
  68.0 0.7 %copy.10 = f32[1,4,64,256]{3,2,1,0:T(8,128)} copy(f32[1,4,64,256]{3,2,1,0:T(8,128)S(1)} %copy-done) | data formatting | bytes 524288
Async XLA Ops:
  66.3 1.7 %copy-start = (f32[1,4,64,256]{3,2,1,0:T(8,128)S(1)}, f32[1,4,64,256]{3,2,1,0:T(8,128)}, u32[]{:S(2)}) copy-start(f32[1,4,64,256]{3,2,1,0:T(8,128)} %get-tuple-element.5) | copy-start | bytes 786436

commit v3 on v2

--- a/solution.py
+++ b/solution.py
@@ -11,14 +11,24 @@
 CG_COARSE = 4
 PARA_ITERS = 2
 MESH = pl.DeviceIdType.MESH
-HIGH = lax.Precision.HIGHEST
 F32 = jnp.float32
+BF16 = jnp.bfloat16
+
+
+def pieces(x):
+    first = x.astype(BF16)
+    x = x - first.astype(F32)
+    second = x.astype(BF16)
+    return first, second, (x - second.astype(F32)).astype(BF16)
 
 
 def dot(a, b):
-    return lax.dot_general(
-        a, b, (((1,), (0,)), ((), ())), precision=HIGH, preferred_element_type=F32
+    left = pieces(a) if a.dtype == F32 else (a,) * 3
+    right = pieces(b) if b.dtype == F32 else (b,) * 3
+    first, second, third = (
+        jnp.dot(x, y, preferred_element_type=F32) for x, y in zip(left, right)
     )
+    return first + (second + third)
 
 
 def kernel(
@@ -81,17 +91,17 @@
     rowi = lax.broadcasted_iota(jnp.int32, (NY, NZ), 0)
     coli = lax.broadcasted_iota(jnp.int32, (NY, NZ), 1)
     ey = (lax.broadcasted_iota(jnp.int32, (NY // 4, NY), 1) // 4
-          == lax.broadcasted_iota(jnp.int32, (NY // 4, NY), 0)).astype(F32)
+          == lax.broadcasted_iota(jnp.int32, (NY // 4, NY), 0)).astype(F32).astype(BF16)
     eyt = (lax.broadcasted_iota(jnp.int32, (NY, NY // 4), 0) // 4
-           == lax.broadcasted_iota(jnp.int32, (NY, NY // 4), 1)).astype(F32)
+           == lax.broadcasted_iota(jnp.int32, (NY, NY // 4), 1)).astype(F32).astype(BF16)
     zr = lax.broadcasted_iota(jnp.int32, (NZ, 2 * hl), 0) // 4
     zc = lax.broadcasted_iota(jnp.int32, (NZ, 2 * hl), 1)
-    down_lo = (zr == zc).astype(F32)
-    down_hi = (zr == zc - hl).astype(F32)
+    down_lo = (zr == zc).astype(F32).astype(BF16)
+    down_hi = (zr == zc - hl).astype(F32).astype(BF16)
     tr = lax.broadcasted_iota(jnp.int32, (2 * hl, NZ), 0)
     tc = lax.broadcasted_iota(jnp.int32, (2 * hl, NZ), 1) // 4
-    up_lo = (tr == tc).astype(F32)
-    up_hi = (tr - hl == tc).astype(F32)
+    up_lo = (tr == tc).astype(F32).astype(BF16)
+    up_hi = (tr - hl == tc).astype(F32).astype(BF16)
 
     def restrict4(total):
         t = dot(ey, total)
@@ -205,7 +215,8 @@
         return 0.0625 * (6.0 * c - ((xs + za) + (zb + ya) + yb))
 
     def total3(x):
-        return jnp.sum(jnp.sum(x, axis=0), keepdims=True).reshape(1, 1, 1)
+        y = jnp.sum(jnp.sum(x, axis=0), axis=0, keepdims=True)
+        return jnp.sum(y, axis=1, keepdims=True)[None]
 
     def solve(i, c):
         source = cur[i, 0:1, :][None] * setup[:, 2]
@@ -259,7 +270,7 @@
             R[i + 1] = jnp.where(inside, r, 0.0)
             return carry
 
-        lax.fori_loop(0, lx + 3, step, 0)
+        lax.fori_loop(0, lx + 3, step, 0, unroll=True)
 
         def step_v(i, carry):
             g = s * lx + i
@@ -268,7 +279,7 @@
             V[i + 2] = jnp.where(g < S * lx, v, 0.0)
             return carry
 
-        lax.fori_loop(0, lx + 1, step_v, 0)
+        lax.fori_loop(0, lx + 1, step_v, 0, unroll=True)
 
     def fold(x):
         y = x[:, :2 * hl]
@@ -289,7 +300,7 @@
             return (m0 + fold(r * r), m1 + fold(r * v), m2 + fold(v * v), m3 + fold(v * av))
 
         z8 = jnp.zeros((8, 2 * hl), F32)
-        ms = lax.fori_loop(0, lx, step, (z8, z8, z8, z8))
+        ms = lax.fori_loop(0, lx, step, (z8, z8, z8, z8), unroll=True)
         block = jnp.zeros((8, 2 * hl), F32)
         for j, m in enumerate(ms):
             block = jnp.where(row8 == j, jnp.sum(m, axis=0, keepdims=True), block)
@@ -357,7 +368,7 @@
             U[i] = U[i] + a * R[i] + b * V[i]
             return carry
 
-        lax.fori_loop(0, lx + 5, update, 0)
+        lax.fori_loop(0, lx + 5, update, 0, unroll=True)
         fine_residual(1, sl)
         fine_moments(2 * k + 1)
         a, b = fine_coefficients(2 * k + 1)

time: 68.9 us -> 62.8 us (0.911)
  Pallas kernels: 65.6 us -> 59.1 us
    pallas_call x1, Pallas kernels: 65.6 us -> 59.1 us  [body(): pl.pallas_call(functools.partial(kernel, T, S, lx), out_shape=(shape, sha...]
where the time goes in v3:
time: 62.8 us; the launch traced here: 62.2 us
  Pallas kernels  59.1 us (94%)
  local copies, waits for them, and re-layouts  2.42 us (4%)
  between operations  0.65 us (1%)
    pallas_call x1, Pallas kernels, body(): pl.pallas_call(functools.partial(kernel, T, S, lx), out_shape=(shape, sha...  59.1 us
    unnamed x4, local copies, waits for them, and re-layouts  2.42 us

profile of v3, /device:TPU:0, one launch (start us, length us, event | category | flops | bytes accessed | tf_op | source)
XLA Modules:
  0.0 62.2 jit_solution(785485544197789030)
XLA Ops:
  0.6 59.1 %shard_map.68 = (f32[1,4,64,256]{3,2,1,0:T(8,128)}, f32[1,4,64,256]{3,2,1,0:T(8,128)}) custom-call(s32[4,64,256]{2,1,0:T(8,128)} %labels_in.1, f32[4]{0:T(128)} %cond.1, f32[3,4,64,256]{3,2,1,0:T(8,128)} %coil_in.1, f32[1,2,3]{2,1,0:T(2,128)} %currents.1, f32[4,64,256]{2,1,0:T(8,128)} %init_in.1), custom_call_target="tpu_custom_call" | custom-call | tf_op jit(solution)/shard_map/pallas_call | solution.py:555
  59.7 0.0 copy-start
  59.7 1.7 %copy.9 = f32[1,4,64,256]{3,2,1,0:T(8,128)} copy(f32[1,4,64,256]{3,2,1,0:T(8,128)} %get-tuple-element.4) | data formatting | bytes 524288
  61.5 0.0 copy-done
  61.5 0.7 %copy.10 = f32[1,4,64,256]{3,2,1,0:T(8,128)} copy(f32[1,4,64,256]{3,2,1,0:T(8,128)S(1)} %copy-done) | data formatting | bytes 524288
Async XLA Ops:
  59.7 1.7 %copy-start = (f32[1,4,64,256]{3,2,1,0:T(8,128)S(1)}, f32[1,4,64,256]{3,2,1,0:T(8,128)}, u32[]{:S(2)}) copy-start(f32[1,4,64,256]{3,2,1,0:T(8,128)} %get-tuple-element.5) | copy-start | bytes 786436
